TPU v7x, 256 devices: a whole 4x4x8 slice. The times are simulated.
256 devices in a mesh: det: 64 (over x, z, core), row: 4 (over y).
Axes of the slice: x: 4, y: 4, z: 8, core: 2. Of those that a mesh axis runs over, the one named last changes fastest.
Arguments:
- images: bfloat16 [384, 3, 384, 384], P('det', None, 'row'), may hold values from -6 to 6
- warp_rows: bfloat16 [384, 3, 384, 384], P('det', None, 'row'), may hold values from -0.3125 to 0.3125
- warp_cols: bfloat16 [384, 3, 384, 384], P('det'), may hold values from -0.3125 to 0.3125
- psf_coef: float32 [384, 3, 21], P('det'), may hold values from -1.25 to 1.25
- taps: float32 [21, 21], replicated, may hold values from -1.25 to 1.25
- dest_patch: int32 [3456, 1], replicated, may hold values from 0 to 63; in each aligned block of 54 rows (0 to 53, 54 to 107, ...) at most 2 rows name the same one
- dest_block: int32 [3456], replicated, may hold values from 0 to 2
- weight_index: int32 [384, 3], replicated, may hold values from 0 to 7
- weight_table: float32 [8], replicated, may hold values from 0.25 to 4
- patch_home: int32 [64], replicated, may hold values from 0 to 63, each once
Outputs:
- difference: bfloat16 [384, 3, 384, 384], P('det', None, 'row')
- coadd: bfloat16 [64, 384, 384], P('det', 'row')
Inputs may be any that keep to these rules, and one draw needn't show every extreme that they name: `dest_patch`: within the 54 rows of one device (an aligned block of rows), no patch is named more than 2 times. `patch_home`: each position once.
All inputs are finite; a program needn't handle non-finite values.
Results may differ from a plain program's by a relative error of at most 0.0082.
Values may be sent and summed in bfloat16 or wider, within the bound.
A program may use at most 128 MiB of HBM per device.

v0:
```python
import jax
import jax.numpy as jnp
from jax import lax
from jax.sharding import PartitionSpec as P

TILE = 128


def extended(value, sides, width):
    for axis, dim in sides:
        size, length = (lax.axis_size(axis), value.shape[dim])
        up = [(i, (i + 1) % size) for i in range(size - 1)]
        down = [(j, i) for i, j in up]
        last = lax.slice_in_dim(value, length - width, length, axis=dim)
        first = lax.slice_in_dim(value, 0, width, axis=dim)
        before = lax.ppermute(last, axis, up)
        after = lax.ppermute(first, axis, down)
        value = jnp.concatenate([before, value, after], axis=dim)
    return value


def toeplitz_table(values, out_len, in_len):
    span_len = values.shape[1]
    offsets = jnp.arange(in_len)[None, :] - jnp.arange(out_len)[:, None]
    picks = (offsets[:, :, None] == jnp.arange(span_len)[None, None, :]).astype(jnp.float32)
    return jnp.einsum("oij,kj->koi", picks, values.astype(jnp.float32)).astype(jnp.bfloat16)


def per_device(
    images,
    warp_rows,
    warp_cols,
    psf_coef,
    taps,
    dest_patch,
    dest_block,
    weight_index,
    weight_table,
    patch_home,
):
    det_count, visit_count, band_rows, side_cols = images.shape
    kernel_count, tap_count = taps.shape
    reach = (tap_count - 1) // 2
    tile_cols = TILE
    tile_count = side_cols // tile_cols
    det_devices = lax.axis_size("det")
    my_index = lax.axis_index("det")
    image_count = det_count * visit_count
    piece_count = image_count * tile_count
    capacity = max(2, 2 * ((piece_count + det_devices - 1) // det_devices))
    slot_count = det_devices * capacity
    padded_rows = band_rows + 2 * reach
    col_warped = jnp.einsum(
        "dvbs,dvst->dvbt", images, warp_cols, preferred_element_type=jnp.float32
    ).astype(jnp.bfloat16)
    warped = jnp.einsum(
        "dvbr,dvrs->dvbs",
        warp_rows,
        lax.all_gather(col_warped, "row", axis=2, tiled=True),
        preferred_element_type=jnp.float32,
    ).astype(jnp.bfloat16)
    padded = extended(warped, (("row", 2),), reach)
    taps_half = taps.astype(jnp.bfloat16)
    col_table = toeplitz_table(taps_half, tile_cols, tile_cols + 2 * reach)
    tiles_in = padded.reshape(image_count, padded_rows, side_cols)
    coef_rows = psf_coef.reshape(image_count, kernel_count)

    def match_image(inputs):
        tile_image, coef_row = inputs
        widened = jnp.pad(tile_image, ((0, 0), (reach, reach)))
        windows = jnp.stack(
            [
                widened[
                    :, column_tile * tile_cols : column_tile * tile_cols + tile_cols + 2 * reach
                ]
                for column_tile in range(tile_count)
            ],
            axis=1,
        )
        conv_cols = jnp.einsum(
            "rtw,kcw->krtc", windows, col_table, preferred_element_type=jnp.float32
        ).astype(jnp.bfloat16)
        conv_cols = conv_cols.reshape(kernel_count, padded_rows, side_cols)
        scaled = (coef_row[:, None] * taps).astype(jnp.bfloat16)
        row_table = toeplitz_table(scaled, band_rows, padded_rows)
        return jnp.einsum("kbr,krs->bs", row_table, conv_cols, preferred_element_type=jnp.float32)

    matched = lax.map(match_image, (tiles_in, coef_rows))
    level_count = weight_table.shape[0]
    level_onehot = (weight_index[:, :, None] == jnp.arange(level_count)[None, None, :]).astype(
        jnp.float32
    )
    weight_all = jnp.sum(level_onehot * weight_table[None, None, :], axis=2)
    weight_mine = lax.dynamic_slice_in_dim(weight_all, my_index * det_count, det_count, 0).reshape(
        image_count
    )
    weighted = (
        (weight_mine[:, None, None] * matched)
        .astype(jnp.bfloat16)
        .reshape(image_count, band_rows, tile_count, tile_cols)
    )
    patch_count = patch_home.shape[0]
    patch_ids = dest_patch[:, 0]
    owner_all = jnp.sum(
        jnp.where(patch_ids[:, None] == jnp.arange(patch_count)[None, :], patch_home[None, :], 0),
        axis=1,
    )
    owner_grid = owner_all.reshape(det_devices, piece_count)
    earlier = jnp.arange(piece_count)[None, :] < jnp.arange(piece_count)[:, None]
    rank_grid = jnp.sum(
        ((owner_grid[:, :, None] == owner_grid[:, None, :]) & earlier[None]).astype(jnp.int32),
        axis=2,
    )
    slot_grid = owner_grid * capacity + rank_grid
    slot_mine = lax.dynamic_slice_in_dim(slot_grid, my_index, 1, 0)[0]
    send_pick = (
        (jnp.arange(slot_count)[:, None] == slot_mine[None, :])
        .astype(jnp.bfloat16)
        .reshape(slot_count, image_count, tile_count)
    )
    weight_pieces = jnp.repeat(weight_all.reshape(-1), tile_count)
    to_mine = owner_all == my_index
    block_onehot = (dest_block[:, None] == jnp.arange(tile_count)[None, :]).astype(jnp.float32)
    denominator = jnp.sum(
        jnp.where(to_mine[:, None], block_onehot * weight_pieces[:, None], 0.0), axis=0
    )
    source_slot = jnp.arange(
        det_devices * piece_count
    ) // piece_count * capacity + rank_grid.reshape(-1)
    slot_onehot = (
        (source_slot[:, None] == jnp.arange(slot_count)[None, :]) & to_mine[:, None]
    ).astype(jnp.float32)
    gather_matrix = jnp.einsum("iq,is->qs", block_onehot, slot_onehot).astype(jnp.bfloat16)
    outgoing = jnp.einsum(
        "spq,pbqc->sbc", send_pick, weighted, preferred_element_type=jnp.float32
    ).astype(jnp.bfloat16)
    received = lax.all_to_all(outgoing, "det", split_axis=0, concat_axis=0, tiled=True)
    numerator = jnp.einsum(
        "qs,sbc->bqc", gather_matrix, received, preferred_element_type=jnp.float32
    )
    template = (numerator / jnp.maximum(denominator, 1.0)[None, :, None]).astype(jnp.bfloat16)
    coadd_band = template.reshape(1, band_rows, side_cols)
    returned = jnp.einsum(
        "qs,bqc->sbc", gather_matrix, template, preferred_element_type=jnp.float32
    ).astype(jnp.bfloat16)
    arrived = lax.all_to_all(returned, "det", split_axis=0, concat_axis=0, tiled=True)
    local_template = jnp.einsum(
        "spq,sbc->pbqc", send_pick, arrived, preferred_element_type=jnp.float32
    )
    difference = (
        matched.reshape(image_count, band_rows, tile_count, tile_cols) - local_template
    ).astype(jnp.bfloat16)
    difference = difference.reshape(det_count, visit_count, band_rows, side_cols)
    return (difference, coadd_band)


def solution(mesh):
    placed = (
        P("det", None, "row", None),
        P("det", None, "row", None),
        P("det", None, None, None),
        P("det", None, None),
        P(),
        P(),
        P(),
        P(),
        P(),
        P(),
    )
    return jax.shard_map(
        per_device,
        mesh=mesh,
        in_specs=placed,
        out_specs=(P("det", None, "row", None), P("det", "row", None)),
        check_vma=False,
    )
```

profile of v0, /device:TPU:1, one launch (start us, length us, event | category | flops | bytes accessed | tf_op | source)
XLA Modules:
  0.0 490.7 jit_solution(14183806398760456192)
XLA Ops:
  8.5 4.7 convolution_convert_fusion.3
  15.2 62.1 %all-gather.2.cloned.1.call-done = bf16[6,3,384,384]{3,2,1,0:T(8,128)(2,1)} async-done(((bf16[6,3,96,384]{3,2,1,0:T(8,128)(2,1)}), bf16[6,3,384,384]{3,2,1,0:T(8,128)(2,1)}) %all-gather.2.cloned.1.call-update) | async-done | bytes 5308432 | tf_op jit(solution)/shard_map/all_gather | solution.py:59
  77.3 3.6 fusion.26
  87.8 3.8 collective-permute-done.1
  93.4 198.1 %while.12 = (s32[]{:T(128)}, f32[18,96,384]{2,1,0:T(8,128)}, f32[18,21]{1,0:T(8,128)S(1)}, f32[21,21]{1,0:T(8,128)S(1)}, bf16[18,116,384]{2,1,0:T(8,128)(2,1)}, /*index=5*/bf16[21,128,148]{1,2,0:T(8,128)(2,1)}, s32[]{:T(128)}) while((s32[]{:T(128)}, f32[18,96,384]{2,1,0:T(8,128)}, f32[18,21]{1,0:T(8,128)S(1)}, f32[21,21]{1,0:T(8,128)S(1)}, ...), condition=%wide.region_1.2_spmd, body=%wide.region_0.1_spmd.sunk | while | flops 468033056 | bytes 10274817 | solution.py:88
  95.7 3.2 convert_bitcast_fusion.2
  98.9 3.0 copy.109
  106.7 3.2 convert_bitcast_fusion.2
  109.9 3.0 copy.109
  117.7 3.2 convert_bitcast_fusion.2
  120.9 3.0 copy.109
  128.7 3.2 convert_bitcast_fusion.2
  131.9 3.0 copy.109
  139.7 3.2 convert_bitcast_fusion.2
  142.9 3.0 copy.109
  150.7 3.2 convert_bitcast_fusion.2
  153.9 3.0 copy.109
  161.7 3.2 convert_bitcast_fusion.2
  164.9 3.0 copy.109
  172.7 3.2 convert_bitcast_fusion.2
  175.9 3.0 copy.109
  183.7 3.2 convert_bitcast_fusion.2
  186.9 3.0 copy.109
  194.7 3.2 convert_bitcast_fusion.2
  197.9 3.0 copy.109
  205.7 3.2 convert_bitcast_fusion.2
  216.7 3.2 convert_bitcast_fusion.2
  219.9 3.0 copy.109
  227.7 3.2 convert_bitcast_fusion.2
  230.9 3.0 copy.109
  238.7 3.2 convert_bitcast_fusion.2
  241.9 3.0 copy.109
  249.7 3.2 convert_bitcast_fusion.2
  252.9 3.0 copy.109
  260.7 3.2 convert_bitcast_fusion.2
  263.9 3.0 copy.109
  271.7 3.2 convert_bitcast_fusion.2
  274.9 3.0 copy.109
  282.7 3.2 convert_bitcast_fusion.2
  291.5 3.1 multiply_convert_fusion.1
  294.5 3.6 reshape.134
  300.1 3.7 copy.71
  303.8 12.1 %all-to-all-start = ((bf16[128,96,128]{2,1,0:T(8,128)(2,1)}), bf16[128,96,128]{2,1,0:T(8,128)(2,1)}, u32[]{:S(2)}, u32[]{:S(2)}) async-start(bf16[128,96,128]{2,1,0:T(8,128)(2,1)} %copy.71), calls=%async_computation | async-start | bytes 6291456 | tf_op jit(solution)/shard_map/all_to_all | solution.py:137
  318.4 71.0 %all-to-all-done = bf16[128,96,128]{2,1,0:T(8,128)(2,1)} async-done(((bf16[128,96,128]{2,1,0:T(8,128)(2,1)}), bf16[128,96,128]{2,1,0:T(8,128)(2,1)}, u32[]{:S(2)}, u32[]{:S(2)}) %all-to-all-start) | async-done | bytes 3145760 | tf_op jit(solution)/shard_map/all_to_all | solution.py:137
  393.3 3.7 copy.74
  397.0 6.2 %all-to-all-start.1 = ((bf16[128,96,128]{2,1,0:T(8,128)(2,1)}), bf16[128,96,128]{2,1,0:T(8,128)(2,1)}, u32[]{:S(2)}, u32[]{:S(2)}) async-start(bf16[128,96,128]{2,1,0:T(8,128)(2,1)} %copy.74), calls=%async_computation.1 | async-start | bytes 6291456 | tf_op jit(solution)/shard_map/all_to_all | solution.py:146
  403.9 72.7 %all-to-all-done.1 = bf16[128,96,128]{2,1,0:T(8,128)(2,1)} async-done(((bf16[128,96,128]{2,1,0:T(8,128)(2,1)}), bf16[128,96,128]{2,1,0:T(8,128)(2,1)}, u32[]{:S(2)}, u32[]{:S(2)}) %all-to-all-start.1) | async-done | bytes 3145760 | tf_op jit(solution)/shard_map/all_to_all | solution.py:146
  476.7 3.3 fusion.15
  (191 shorter events, 116.4 us)
Async XLA Ops:
  7.2 1.3 copy-start
  7.2 6.1 %copy-start.9 = (f32[8]{0:T(128)S(1)}, f32[8]{0:T(128)}, u32[]{:S(2)}) copy-start(f32[8]{0:T(128)} %param.20) | copy-start | bytes 100
  7.2 6.1 %copy-start.7 = (s32[384,3]{0,1:T(4,128)S(1)}, s32[384,3]{0,1:T(4,128)}, u32[]{:S(2)}) copy-start(s32[384,3]{0,1:T(4,128)} %param.19) | copy-start | bytes 13828
  7.2 6.4 %copy-start.6 = (f32[6,3,21]{2,1,0:T(4,128)S(1)}, f32[6,3,21]{2,1,0:T(4,128)}, u32[]{:S(2)}) copy-start(f32[6,3,21]{2,1,0:T(4,128)} %param.15) | copy-start | bytes 4540
  7.2 6.4 %copy-start.5 = (s32[3456,1]{0,1:T(1,128)S(1)}, s32[3456,1]{0,1:T(1,128)}, u32[]{:S(2)}) copy-start(s32[3456,1]{0,1:T(1,128)} %param.17) | copy-start | bytes 41476
  7.2 6.5 %copy-start.8 = (s32[64]{0:T(128)S(1)}, s32[64]{0:T(128)}, u32[]{:S(2)}) copy-start(s32[64]{0:T(128)} %param.21) | copy-start | bytes 772
  7.2 70.1 %all-gather.2.cloned.1.call-start = ((), (), s32[]{:S(2)}) async-start(), calls=%async_computation.2 | async-start | bytes 6635520 | tf_op jit(solution)/shard_map/all_gather | solution.py:59
  13.2 64.1 %copy-start.2 = (bf16[6,3,96,384]{3,2,1,0:T(8,128)(2,1)S(1)}, bf16[6,3,96,384]{3,2,1,0:T(8,128)(2,1)}, u32[]{:S(2)}) copy-start(bf16[6,3,96,384]{3,2,1,0:T(8,128)(2,1)} %param.13) | copy-start | bytes 3981316
  15.2 69.8 %copy-start.3 = (f32[21,21]{1,0:T(8,128)S(1)}, f32[21,21]{1,0:T(8,128)}, u32[]{:S(2)}) copy-start(f32[21,21]{1,0:T(8,128)} %param.16) | copy-start | bytes 5296
  81.0 6.7 %collective-permute-start = (bf16[6,3,10,384]{3,2,1,0:T(8,128)(2,1)S(1)}, bf16[6,3,10,384]{3,2,1,0:T(8,128)(2,1)S(1)}, u32[]{:S(2)}, u32[]{:S(2)}) collective-permute-start(bf16[6,3,10,384]{3,2,1,0:T(8,128)(2,1)S(1)} %get-tuple-element.125), channel_id=1, source_target_pairs={{0,1},{1,2},{2,3},{4,5},{5,6},{6,7},{8,9},{9,10},{10,11},{12,13},{... | collective-permute-start | bytes 414728 | tf_op jit(solution)/shard_map/ppermute | solution.py:16
  83.7 7.9 %collective-permute-start.1 = (bf16[6,3,10,384]{3,2,1,0:T(8,128)(2,1)S(1)}, bf16[6,3,10,384]{3,2,1,0:T(8,128)(2,1)S(1)}, u32[]{:S(2)}, u32[]{:S(2)}) collective-permute-start(bf16[6,3,10,384]{3,2,1,0:T(8,128)(2,1)S(1)} %get-tuple-element.126), channel_id=1, source_target_pairs={{1,0},{2,1},{3,2},{5,4},{6,5},{7,6},{9,8},{10,9},{11,10},{13,12},{... | collective-permute-start | bytes 414728 | tf_op jit(solution)/shard_map/ppermute | solution.py:17
  303.8 13.3 %copy-start.4 = (s32[3456]{0:T(1024)S(1)}, s32[3456]{0:T(1024)}, u32[]{:S(2)}) copy-start(s32[3456]{0:T(1024)} %param.18) | copy-start | bytes 41476
  303.8 85.6 %all-to-all-start = ((bf16[128,96,128]{2,1,0:T(8,128)(2,1)}), bf16[128,96,128]{2,1,0:T(8,128)(2,1)}, u32[]{:S(2)}, u32[]{:S(2)}) async-start(bf16[128,96,128]{2,1,0:T(8,128)(2,1)} %copy.71), calls=%async_computation | async-start | bytes 6291456 | tf_op jit(solution)/shard_map/all_to_all | solution.py:137
  397.0 79.7 %all-to-all-start.1 = ((bf16[128,96,128]{2,1,0:T(8,128)(2,1)}), bf16[128,96,128]{2,1,0:T(8,128)(2,1)}, u32[]{:S(2)}, u32[]{:S(2)}) async-start(bf16[128,96,128]{2,1,0:T(8,128)(2,1)} %copy.74), calls=%async_computation.1 | async-start | bytes 6291456 | tf_op jit(solution)/shard_map/all_to_all | solution.py:146
  476.7 3.3 copy-start.1
Sparse Core Ops, SparseCore 0:
  13.4 63.8 all-gather.1
where the time goes:
time: 495 us; the launch traced here: 491 us
  waiting for transfers between devices  211 us (43%)
  matrix products  143 us (29%)
  local copies, waits for them, and re-layouts  92.9 us (19%)
  starting transfers between devices  22.4 us (5%)
  between operations  14.4 us (3%)
  other arithmetic  7.01 us (1%)
    all_to_all x1, waiting for transfers between devices, per_device(): lax.all_to_all(returned, 'det', split_axis=0, concat_axis=0, tiled=True)  72.7 us
    all_to_all x1, waiting for transfers between devices, per_device(): lax.all_to_all(outgoing, 'det', split_axis=0, concat_axis=0, tiled=True)  71 us
    all_gather x1, waiting for transfers between devices, per_device(): lax.all_gather(col_warped, 'row', axis=2, tiled=True)  62.1 us
    dot_general x18, matrix products, match_image(): jnp.einsum('rtw,kcw->krtc', windows, col_table, preferred_element_type=jn...  57.4 us
    convert_element_type x18, local copies, waits for them, and re-layouts, match_image(): conv_cols = jnp.einsum('rtw,kcw->krtc', windows, col_table, preferred_ele...  54.3 us
    dot_general x18, matrix products, match_image(): jnp.einsum('kbr,krs->bs', row_table, conv_cols, preferred_element_type=jn...  44.7 us
    dot_general x19, matrix products, toeplitz_table(): jnp.einsum('oij,kj->koi', picks, values.astype(jnp.float32))  22.1 us
    dynamic_slice x36, local copies, waits for them, and re-layouts, per_device(): matched = lax.map(match_image, (tiles_in, coef_rows))  18.7 us
  transfers between devices with their start and end apart: 5, of which 5 were waited for; matrix products, arithmetic and copies ran while one was open for 1% of the time, Pallas kernels for 0%

commit v1 on v0

--- a/solution.py
+++ b/solution.py
@@ -53,11 +53,35 @@
     col_warped = jnp.einsum(
         "dvbs,dvst->dvbt", images, warp_cols, preferred_element_type=jnp.float32
     ).astype(jnp.bfloat16)
-    warped = jnp.einsum(
-        "dvbr,dvrs->dvbs",
-        warp_rows,
-        lax.all_gather(col_warped, "row", axis=2, tiled=True),
-        preferred_element_type=jnp.float32,
+
+    def end_runs_over_axis(here_x, named_axis, packet):
+        local_out, main, v_next = (
+            lax.psum(1, named_axis),
+            lax.axis_index(named_axis),
+            here_x.shape[2],
+        )
+        inbox = [(to_i, (to_i + 1) % local_out) for to_i in range(local_out)]
+        opened = local_out // 2
+        outcome_arr = known = here_x
+        met_up = packet(here_x, main * v_next)
+        samples = [(to_i, (to_i - 1) % local_out) for to_i in range(local_out)]
+        for p in range(1, opened + 1):
+            outcome_arr = lax.ppermute(outcome_arr, named_axis, inbox)
+            if p < local_out - opened:
+                known = lax.ppermute(known, named_axis, samples)
+                met_up = met_up + packet(known, (main + p) % local_out * v_next)
+            met_up = met_up + packet(outcome_arr, (main - p) % local_out * v_next)
+        return met_up
+
+    warped = end_runs_over_axis(
+        col_warped,
+        "row",
+        lambda own_block, at: jnp.einsum(
+            "dvbr,dvrs->dvbs",
+            lax.dynamic_slice_in_dim(warp_rows, at, own_block.shape[2], axis=3),
+            own_block,
+            preferred_element_type=jnp.float32,
+        ),
     ).astype(jnp.bfloat16)
     padded = extended(warped, (("row", 2),), reach)
     taps_half = taps.astype(jnp.bfloat16)

time: 495 us -> 444 us (0.90)
  matrix products: 143 us -> 111 us
  waiting for transfers between devices: 211 us -> 197 us
  between operations: 14.4 us -> 0.97 us
  starting transfers between devices: 22.4 us -> 32 us
    all_gather x1 -> x0, waiting for transfers between devices: 62.1 us -> none  [per_device(): lax.all_gather(col_warped, 'row', axis=2, tiled=True)]
    ppermute x0 -> x3, waiting for transfers between devices: none -> 48.3 us  [the longest x2 48.3 us: end_runs_over_axis(): outcome_arr = lax.ppermute(outcome_arr, named_axis, inbox)]
    dot_general x18, matrix products: 44.7 us -> 25.4 us  [match_image(): jnp.einsum('kbr,krs->bs', row_table, conv_cols, preferred_element_type=jn...]
    dot_general x19, matrix products: 22.1 us -> 7.15 us  [toeplitz_table(): jnp.einsum('oij,kj->koi', picks, values.astype(jnp.float32))]
    ppermute x0 -> x3, starting transfers between devices: none -> 5.29 us  [the longest x2 3.76 us: end_runs_over_axis(): outcome_arr = lax.ppermute(outcome_arr, named_axis, inbox)]
  transfers between devices with their start and end apart: 5 -> 7, of which waited for: 5 -> 6; matrix products, arithmetic and copies ran while one was open for 1% -> 2% of each run, Pallas kernels for 0% -> 0%
where the time goes in v1:
time: 444 us; the launch traced here: 441 us
  waiting for transfers between devices  197 us (44%)
  matrix products  111 us (25%)
  local copies, waits for them, and re-layouts  91.6 us (21%)
  starting transfers between devices  32 us (7%)
  other arithmetic  7.94 us (2%)
    all_to_all x1, waiting for transfers between devices, per_device(): lax.all_to_all(returned, 'det', split_axis=0, concat_axis=0, tiled=True)  72.7 us
    all_to_all x1, waiting for transfers between devices, per_device(): lax.all_to_all(outgoing, 'det', split_axis=0, concat_axis=0, tiled=True)  71 us
    dot_general x18, matrix products, match_image(): jnp.einsum('rtw,kcw->krtc', windows, col_table, preferred_element_type=jn...  57.2 us
    convert_element_type x18, local copies, waits for them, and re-layouts, match_image(): conv_cols = jnp.einsum('rtw,kcw->krtc', windows, col_table, preferred_ele...  54.3 us
    ppermute x2, waiting for transfers between devices, end_runs_over_axis(): outcome_arr = lax.ppermute(outcome_arr, named_axis, inbox)  48.3 us
    dot_general x18, matrix products, match_image(): jnp.einsum('kbr,krs->bs', row_table, conv_cols, preferred_element_type=jn...  25.4 us
    dynamic_slice x36, local copies, waits for them, and re-layouts, per_device(): matched = lax.map(match_image, (tiles_in, coef_rows))  18.5 us
    all_to_all x1, starting transfers between devices, per_device(): lax.all_to_all(outgoing, 'det', split_axis=0, concat_axis=0, tiled=True)  16.2 us
  transfers between devices with their start and end apart: 7, of which 6 were waited for; matrix products, arithmetic and copies ran while one was open for 2% of the time, Pallas kernels for 0%

profile of v1, /device:TPU:1, one launch (start us, length us, event | category | flops | bytes accessed | tf_op | source)
XLA Modules:
  0.0 440.6 jit_solution(10755922324129276715)
XLA Ops:
  0.7 4.2 convolution_convert_fusion.2
  10.3 25.2 %collective-permute-done.1 = bf16[6,3,96,384]{3,2,1,0:T(8,128)(2,1)} collective-permute-done((bf16[6,3,96,384]{3,2,1,0:T(8,128)(2,1)S(1)}, bf16[6,3,96,384]{3,2,1,0:T(8,128)(2,1)}, u32[]{:S(2)}, u32[]{:S(2)}) %collective-permute-start.1) | collective-permute-done | bytes 1327136 | tf_op jit(solution)/shard_map/ppermute | solution.py:69
  42.1 23.2 %collective-permute-done.2 = bf16[6,3,96,384]{3,2,1,0:T(8,128)(2,1)} collective-permute-done((bf16[6,3,96,384]{3,2,1,0:T(8,128)(2,1)}, bf16[6,3,96,384]{3,2,1,0:T(8,128)(2,1)}, u32[]{:S(2)}, u32[]{:S(2)}) %collective-permute-start.2) | collective-permute-done | bytes 1327136 | tf_op jit(solution)/shard_map/ppermute | solution.py:69
  73.2 4.1 collective-permute-done.4
  80.0 164.2 %while.12 = (s32[]{:T(128)}, f32[18,96,384]{2,1,0:T(8,128)}, f32[18,21]{1,0:T(8,128)S(1)}, f32[21,21]{1,0:T(8,128)S(1)}, bf16[18,116,384]{2,1,0:T(8,128)(2,1)}, /*index=5*/bf16[21,128,148]{1,2,0:T(8,128)(2,1)}, s32[]{:T(128)}) while((s32[]{:T(128)}, f32[18,96,384]{2,1,0:T(8,128)}, f32[18,21]{1,0:T(8,128)S(1)}, f32[21,21]{1,0:T(8,128)S(1)}, ...), condition=%wide.region_1.2_spmd, body=%wide.region_0.1_spmd.sunk | while | flops 468033056 | bytes 10153205 | solution.py:112
  81.1 3.2 convert_bitcast_fusion.2
  84.3 3.0 copy.109
  90.2 3.2 convert_bitcast_fusion.2
  93.4 3.0 copy.109
  99.4 3.2 convert_bitcast_fusion.2
  102.5 3.0 copy.109
  108.5 3.2 convert_bitcast_fusion.2
  111.6 3.0 copy.109
  117.6 3.2 convert_bitcast_fusion.2
  126.7 3.2 convert_bitcast_fusion.2
  129.9 3.0 copy.109
  135.8 3.2 convert_bitcast_fusion.2
  139.0 3.0 copy.109
  144.9 3.2 convert_bitcast_fusion.2
  148.1 3.0 copy.109
  154.1 3.2 convert_bitcast_fusion.2
  157.3 3.0 copy.109
  163.2 3.2 convert_bitcast_fusion.2
  166.4 3.0 copy.109
  172.3 3.2 convert_bitcast_fusion.2
  175.5 3.0 copy.109
  181.4 3.2 convert_bitcast_fusion.2
  184.6 3.0 copy.109
  190.5 3.2 convert_bitcast_fusion.2
  193.7 3.0 copy.109
  199.6 3.2 convert_bitcast_fusion.2
  202.8 3.0 copy.109
  208.8 3.2 convert_bitcast_fusion.2
  212.0 3.0 copy.109
  217.9 3.2 convert_bitcast_fusion.2
  221.1 3.0 copy.109
  227.1 3.2 convert_bitcast_fusion.2
  230.2 3.0 copy.109
  236.2 3.2 convert_bitcast_fusion.2
  244.2 3.1 multiply_convert_fusion.1
  247.3 3.6 reshape.134
  252.8 3.7 copy.71
  256.5 16.2 %all-to-all-start = ((bf16[128,96,128]{2,1,0:T(8,128)(2,1)}), bf16[128,96,128]{2,1,0:T(8,128)(2,1)}, u32[]{:S(2)}, u32[]{:S(2)}) async-start(bf16[128,96,128]{2,1,0:T(8,128)(2,1)} %copy.71), calls=%async_computation | async-start | bytes 6291456 | tf_op jit(solution)/shard_map/all_to_all | solution.py:161
  275.2 71.0 %all-to-all-done = bf16[128,96,128]{2,1,0:T(8,128)(2,1)} async-done(((bf16[128,96,128]{2,1,0:T(8,128)(2,1)}), bf16[128,96,128]{2,1,0:T(8,128)(2,1)}, u32[]{:S(2)}, u32[]{:S(2)}) %all-to-all-start) | async-done | bytes 3145760 | tf_op jit(solution)/shard_map/all_to_all | solution.py:161
  350.1 3.7 copy.74
  353.8 6.2 %all-to-all-start.1 = ((bf16[128,96,128]{2,1,0:T(8,128)(2,1)}), bf16[128,96,128]{2,1,0:T(8,128)(2,1)}, u32[]{:S(2)}, u32[]{:S(2)}) async-start(bf16[128,96,128]{2,1,0:T(8,128)(2,1)} %copy.74), calls=%async_computation.1 | async-start | bytes 6291456 | tf_op jit(solution)/shard_map/all_to_all | solution.py:170
  360.7 72.7 %all-to-all-done.1 = bf16[128,96,128]{2,1,0:T(8,128)(2,1)} async-done(((bf16[128,96,128]{2,1,0:T(8,128)(2,1)}), bf16[128,96,128]{2,1,0:T(8,128)(2,1)}, u32[]{:S(2)}, u32[]{:S(2)}) %all-to-all-start.1) | async-done | bytes 3145760 | tf_op jit(solution)/shard_map/all_to_all | solution.py:170
  433.5 3.3 fusion.15
  (195 shorter events, 93.1 us)
Async XLA Ops:
  0.6 37.1 %copy-start = (bf16[6,3,96,384]{3,2,1,0:T(8,128)(2,1)S(1)}, bf16[6,3,96,384]{3,2,1,0:T(8,128)(2,1)}, u32[]{:S(2)}) copy-start(bf16[6,3,96,384]{3,2,1,0:T(8,128)(2,1)} %param.13) | copy-start | bytes 3981316
  0.6 8.0 %copy-start.2 = (f32[21,21]{1,0:T(8,128)S(1)}, f32[21,21]{1,0:T(8,128)}, u32[]{:S(2)}) copy-start(f32[21,21]{1,0:T(8,128)} %param.16) | copy-start | bytes 5296
  4.8 5.3 %copy-start.5 = (f32[6,3,21]{2,1,0:T(4,128)S(1)}, f32[6,3,21]{2,1,0:T(4,128)}, u32[]{:S(2)}) copy-start(f32[6,3,21]{2,1,0:T(4,128)} %param.15) | copy-start | bytes 4540
  4.8 5.3 %copy-start.6 = (s32[384,3]{0,1:T(4,128)S(1)}, s32[384,3]{0,1:T(4,128)}, u32[]{:S(2)}) copy-start(s32[384,3]{0,1:T(4,128)} %param.19) | copy-start | bytes 13828
  4.8 5.3 %copy-start.8 = (f32[8]{0:T(128)S(1)}, f32[8]{0:T(128)}, u32[]{:S(2)}) copy-start(f32[8]{0:T(128)} %param.20) | copy-start | bytes 100
  4.9 32.4 %copy-start.4 = (s32[3456,1]{0,1:T(1,128)S(1)}, s32[3456,1]{0,1:T(1,128)}, u32[]{:S(2)}) copy-start(s32[3456,1]{0,1:T(1,128)} %param.17) | copy-start | bytes 41476
  4.9 32.4 %copy-start.7 = (s32[64]{0:T(128)S(1)}, s32[64]{0:T(128)}, u32[]{:S(2)}) copy-start(s32[64]{0:T(128)} %param.21) | copy-start | bytes 772
  4.9 30.6 %collective-permute-start.1 = (bf16[6,3,96,384]{3,2,1,0:T(8,128)(2,1)S(1)}, bf16[6,3,96,384]{3,2,1,0:T(8,128)(2,1)}, u32[]{:S(2)}, u32[]{:S(2)}) collective-permute-start(bf16[6,3,96,384]{3,2,1,0:T(8,128)(2,1)S(1)} %convolution_convert_fusion.2), channel_id=1, source_target_pairs={{0,1},{1,2},{2,3},{3,0},{4,5},{5,6},{6,7},{7,4},{8,9},{9,10},{10,1... | collective-permute-start | bytes 3981320 | tf_op jit(solution)/shard_map/ppermute | solution.py:69
  7.1 33.2 %collective-permute-start = (bf16[6,3,96,384]{3,2,1,0:T(8,128)(2,1)S(1)}, bf16[6,3,96,384]{3,2,1,0:T(8,128)(2,1)}, u32[]{:S(2)}, u32[]{:S(2)}) collective-permute-start(bf16[6,3,96,384]{3,2,1,0:T(8,128)(2,1)S(1)} %convolution_convert_fusion.2), channel_id=1, source_target_pairs={{0,3},{1,0},{2,1},{3,2},{4,7},{5,4},{6,5},{7,6},{8,11},{9,8},{10,9... | collective-permute-start | bytes 3981320 | tf_op jit(solution)/shard_map/ppermute | solution.py:71
  35.4 29.9 %collective-permute-start.2 = (bf16[6,3,96,384]{3,2,1,0:T(8,128)(2,1)}, bf16[6,3,96,384]{3,2,1,0:T(8,128)(2,1)}, u32[]{:S(2)}, u32[]{:S(2)}) collective-permute-start(bf16[6,3,96,384]{3,2,1,0:T(8,128)(2,1)} %collective-permute-done.1), channel_id=1, source_target_pairs={{0,1},{1,2},{2,3},{3,0},{4,5},{5,6},{6,7},{7,4},{8,9},{9,10},{10,1... | collective-permute-start | bytes 3981320 | tf_op jit(solution)/shard_map/ppermute | solution.py:69
  67.5 5.6 %collective-permute-start.3 = (bf16[6,3,10,384]{3,2,1,0:T(8,128)(2,1)S(1)}, bf16[6,3,10,384]{3,2,1,0:T(8,128)(2,1)S(1)}, u32[]{:S(2)}, u32[]{:S(2)}) collective-permute-start(bf16[6,3,10,384]{3,2,1,0:T(8,128)(2,1)S(1)} %get-tuple-element.125), channel_id=1, source_target_pairs={{0,1},{1,2},{2,3},{4,5},{5,6},{6,7},{8,9},{9,10},{10,11},{12,13},{... | collective-permute-start | bytes 414728 | tf_op jit(solution)/shard_map/ppermute | solution.py:16
  70.3 7.0 %collective-permute-start.4 = (bf16[6,3,10,384]{3,2,1,0:T(8,128)(2,1)S(1)}, bf16[6,3,10,384]{3,2,1,0:T(8,128)(2,1)}, u32[]{:S(2)}, u32[]{:S(2)}) collective-permute-start(bf16[6,3,10,384]{3,2,1,0:T(8,128)(2,1)S(1)} %get-tuple-element.126), channel_id=1, source_target_pairs={{1,0},{2,1},{3,2},{5,4},{6,5},{7,6},{9,8},{10,9},{11,10},{13,12},{... | collective-permute-start | bytes 414728 | tf_op jit(solution)/shard_map/ppermute | solution.py:17
  256.5 17.4 %copy-start.3 = (s32[3456]{0:T(1024)S(1)}, s32[3456]{0:T(1024)}, u32[]{:S(2)}) copy-start(s32[3456]{0:T(1024)} %param.18) | copy-start | bytes 41476
  256.5 89.7 %all-to-all-start = ((bf16[128,96,128]{2,1,0:T(8,128)(2,1)}), bf16[128,96,128]{2,1,0:T(8,128)(2,1)}, u32[]{:S(2)}, u32[]{:S(2)}) async-start(bf16[128,96,128]{2,1,0:T(8,128)(2,1)} %copy.71), calls=%async_computation | async-start | bytes 6291456 | tf_op jit(solution)/shard_map/all_to_all | solution.py:161
  353.8 79.7 %all-to-all-start.1 = ((bf16[128,96,128]{2,1,0:T(8,128)(2,1)}), bf16[128,96,128]{2,1,0:T(8,128)(2,1)}, u32[]{:S(2)}, u32[]{:S(2)}) async-start(bf16[128,96,128]{2,1,0:T(8,128)(2,1)} %copy.74), calls=%async_computation.1 | async-start | bytes 6291456 | tf_op jit(solution)/shard_map/all_to_all | solution.py:170
  433.5 3.3 copy-start.1
